TPU v7x, 512 devices: a whole 4x4x16 slice. The times are simulated.
512 devices in a mesh: lag: 64 (over z, y), par: 8 (over x, core).
Axes of the slice: x: 4, y: 4, z: 16, core: 2. Of those that a mesh axis runs over, the one named last changes fastest.
Arguments:
- prior_rows: bfloat16 [64, 512, 16384], P('lag', None, 'par'), may hold values from -0.0625 to 0.0625
- raw_rows: bfloat16 [64, 512, 16384], P('lag', None, 'par'), may hold values from -6 to 6
Outputs:
- diag_zero: float32 [64, 512, 512], P('lag', 'par')
- diag_one: float32 [64, 512, 512], P('lag', 'par')
All inputs are finite; a program needn't handle non-finite values.
Results may differ from a plain program's by a relative error of at most 0.0003.
Values may be sent and summed in bfloat16 or wider, within the bound.
No kernel may reach another device: no remote copies, remote signals or barrier semaphores. Data moves between devices by JAX's collectives and lax.ppermute only.
A program may use at most 64 MiB of HBM per device.

v0:
```python
import jax
import jax.numpy as jnp
from jax import lax
from jax.sharding import PartitionSpec as P


def passed_along(block, axis, distance):
    devices = range(lax.axis_size(axis))
    route = [(i - distance, i) for i in devices if i - distance in devices]
    return lax.ppermute(block, axis, route)


def carried_in(part, axis, combine, identity):
    place = lax.axis_index(axis)
    gathered = lax.all_gather(part, axis)
    state = jnp.zeros_like(part) + jnp.asarray(identity, part.dtype)

    def one(turn, state):
        return combine(state, lax.dynamic_index_in_dim(gathered, turn, 0, False))

    return lax.fori_loop(0, place, one, state)


def add_terms(earlier_term, later_term):
    return earlier_term + later_term


def body(prior_rows, raw_rows):
    incoming = passed_along(raw_rows, "lag", -1)
    following = jnp.concatenate([raw_rows[1:], incoming], axis=0)
    offset_zero = jnp.einsum(
        "lsp,ltp->lst", prior_rows, raw_rows, preferred_element_type=jnp.float32
    )
    offset_one = jnp.einsum(
        "lsp,ltp->lst", prior_rows, following, preferred_element_type=jnp.float32
    )
    stacked = jnp.stack([offset_zero, offset_one], axis=0)
    summed = lax.psum(stacked, "par")
    row_count = summed.shape[2] // lax.axis_size("par")
    shares = lax.dynamic_slice_in_dim(summed, lax.axis_index("par") * row_count, row_count, 2)
    running = jnp.cumsum(shares, axis=1)
    totals = running[:, -1]
    earlier = carried_in(totals, "lag", add_terms, jnp.zeros_like(totals))
    result = running + earlier[:, None]
    return (result[0], result[1])


def solution(mesh):
    in_specs = (P("lag", None, "par"), P("lag", None, "par"))
    out_specs = (P("lag", "par", None), P("lag", "par", None))
    return jax.shard_map(body, mesh=mesh, in_specs=in_specs, out_specs=out_specs, check_vma=False)
```

profile of v0, /device:TPU:504, one launch (start us, length us, event | category | flops | bytes accessed | tf_op | source)
XLA Modules:
  0.0 406.9 jit_solution(13441115809973751010)
XLA Ops:
  7.2 2.9 collective-permute-start
  10.2 2.9 fusion.6
  13.0 42.2 %collective-permute-done = bf16[1,512,2048]{2,1,0:T(8,128)(2,1)S(1)} collective-permute-done((bf16[1,512,2048]{2,1,0:T(8,128)(2,1)}, bf16[1,512,2048]{2,1,0:T(8,128)(2,1)S(1)}, u32[]{:S(2)}, u32[]{:S(2)}) %collective-permute-start) | collective-permute-done | bytes 2097184 | tf_op jit(solution)/shard_map/ppermute | solution.py:10
  55.2 1.3 fusion.11
  56.5 1.5 pad_maximum_fusion
  58.1 83.5 %all-reduce.2.cloned.1.call-done = f32[2,1,512,512]{3,2,1,0:T(8,128)} async-done(((f32[2,1,512,512]{3,2,1,0:T(8,128)}), f32[2,1,512,512]{3,2,1,0:T(8,128)}) %all-reduce.2.cloned.1.call-update) | async-done | bytes 2097168 | tf_op jit(solution)/shard_map/psum | solution.py:38
  141.5 1.7 constant_dynamic-slice_fusion
  143.2 189.3 %all-gather.3.cloned.1.call-done = f32[128,1,64,512]{3,2,1,0:T(8,128)} async-done(((f32[2,1,64,512]{3,2,1,0:T(8,128)}), f32[128,1,64,512]{3,2,1,0:T(8,128)}) %all-gather.3.cloned.1.call-update) | async-done | bytes 16777232 | tf_op jit(solution)/shard_map/all_gather | solution.py:15
  332.6 65.8 %while.10 = (s32[]{:T(128)}, f32[2,64,512]{2,1,0:T(8,128)S(1)}, s32[]{:T(128)}, f32[64,2,64,512]{3,2,1,0:T(8,128)}, s32[]{:T(128)}, /*index=5*/s32[]{:T(128)}, s32[]{:T(128)}) while((s32[]{:T(128)}, f32[2,64,512]{2,1,0:T(8,128)S(1)}, s32[]{:T(128)}, f32[64,2,64,512]{3,2,1,0:T(8,128)}, s32[]{:T(128)}, /*index=5*/s32[]{:T(128)}, s32[]{:T(128)}) %tuple.30), condition=%wide.region_2.3_spmd, body=%wide.region_1.0_spmd.sunk | while | flops 65541 | bytes 786555 | solution.py:21
  332.6 1.0 bitcast_add_fusion.3
  333.6 1.0 bitcast_add_fusion.3
  334.7 1.0 bitcast_add_fusion.3
  335.7 1.0 bitcast_add_fusion.3
  336.8 1.0 bitcast_add_fusion.3
  337.8 1.0 bitcast_add_fusion.3
  338.9 1.0 bitcast_add_fusion.3
  339.9 1.0 bitcast_add_fusion.3
  345.1 1.0 bitcast_add_fusion.3
  347.2 1.0 bitcast_add_fusion.3
  349.3 1.0 bitcast_add_fusion.3
  351.4 1.0 bitcast_add_fusion.3
  353.5 1.0 bitcast_add_fusion.3
  365.0 1.0 bitcast_add_fusion.3
  367.1 1.0 bitcast_add_fusion.3
  369.1 1.0 bitcast_add_fusion.3
  371.2 1.0 bitcast_add_fusion.3
  373.3 1.0 bitcast_add_fusion.3
  384.8 1.0 bitcast_add_fusion.3
  386.9 1.0 bitcast_add_fusion.3
  389.0 1.0 bitcast_add_fusion.3
  391.1 1.0 bitcast_add_fusion.3
  393.2 1.0 bitcast_add_fusion.3
  (49 shorter events, 42.7 us)
Async XLA Ops:
  7.2 3.0 copy-start
  7.2 134.4 %all-reduce.2.cloned.1.call-start = ((), (), s32[]{:S(2)}) async-start(), calls=%async_computation | async-start | bytes 4194304 | tf_op jit(solution)/shard_map/psum | solution.py:38
  7.2 48.0 %collective-permute-start = (bf16[1,512,2048]{2,1,0:T(8,128)(2,1)}, bf16[1,512,2048]{2,1,0:T(8,128)(2,1)S(1)}, u32[]{:S(2)}, u32[]{:S(2)}) collective-permute-start(bf16[1,512,2048]{2,1,0:T(8,128)(2,1)} %param.5), channel_id=1, source_target_pairs={{8,0},{16,8},{24,16},{32,24},{40,32},{48,40},{56,48},{64,56},{72,6... | collective-permute-start | bytes 6291464 | tf_op jit(solution)/shard_map/ppermute | solution.py:10
  58.0 274.5 %all-gather.3.cloned.1.call-start = ((), (), s32[]{:S(2)}) async-start(), calls=%async_computation.1 | async-start | bytes 17039360 | tf_op jit(solution)/shard_map/all_gather | solution.py:15
Sparse Core Ops, SparseCore 0:
  58.2 83.3 all-reduce.1
  144.5 188.0 all-gather.2
where the time goes:
time: 409 us; the launch traced here: 407 us
  waiting for transfers between devices  315 us (77%)
  other arithmetic  66.9 us (16%)
  between operations  14.1 us (3%)
  matrix products  4.16 us (1%)
    all_gather x1, waiting for transfers between devices, carried_in(): gathered = lax.all_gather(part, axis)  189 us
    psum x1, waiting for transfers between devices, body(): summed = lax.psum(stacked, 'par')  83.5 us
    add x63, other arithmetic, add_terms(): return earlier_term + later_term  64.4 us
    ppermute x1, waiting for transfers between devices, passed_along(): return lax.ppermute(block, axis, route)  42.2 us
  transfers between devices with their start and end apart: 3, of which 3 were waited for; matrix products, arithmetic and copies ran while one was open for 1% of the time, Pallas kernels for 0%

commit v1 on v0

--- a/solution.py
+++ b/solution.py
@@ -35,7 +35,7 @@
         "lsp,ltp->lst", prior_rows, following, preferred_element_type=jnp.float32
     )
     stacked = jnp.stack([offset_zero, offset_one], axis=0)
-    summed = lax.psum(stacked, "par")
+    summed = jnp.sum(lax.all_gather(stacked, "par"), axis=0)
     row_count = summed.shape[2] // lax.axis_size("par")
     shares = lax.dynamic_slice_in_dim(summed, lax.axis_index("par") * row_count, row_count, 2)
     running = jnp.cumsum(shares, axis=1)

time: 409 us -> 430 us (1.051)
  waiting for transfers between devices: 315 us -> 326 us
  other arithmetic: 66.9 us -> 76.3 us
    all_gather x0 -> x1, waiting for transfers between devices: none -> 95 us  [body(): summed = jnp.sum(lax.all_gather(stacked, 'par'), axis=0)]
    psum x1 -> x0, waiting for transfers between devices: 83.5 us -> none  [body(): summed = lax.psum(stacked, 'par')]
    reduce_sum x0 -> x1, other arithmetic: none -> 9.43 us  [body(): summed = jnp.sum(lax.all_gather(stacked, 'par'), axis=0)]
where the time goes in v1:
time: 430 us; the launch traced here: 428 us
  waiting for transfers between devices  326 us (76%)
  other arithmetic  76.3 us (18%)
  between operations  14.1 us (3%)
    all_gather x1, waiting for transfers between devices, carried_in(): gathered = lax.all_gather(part, axis)  189 us
    all_gather x1, waiting for transfers between devices, body(): summed = jnp.sum(lax.all_gather(stacked, 'par'), axis=0)  95 us
    add x63, other arithmetic, add_terms(): return earlier_term + later_term  64.4 us
    ppermute x1, waiting for transfers between devices, passed_along(): return lax.ppermute(block, axis, route)  42.2 us
    reduce_sum x1, other arithmetic, body(): summed = jnp.sum(lax.all_gather(stacked, 'par'), axis=0)  9.43 us
  transfers between devices with their start and end apart: 3, of which 3 were waited for; matrix products, arithmetic and copies ran while one was open for 1% of the time, Pallas kernels for 0%

profile of v1, /device:TPU:504, one launch (start us, length us, event | category | flops | bytes accessed | tf_op | source)
XLA Modules:
  0.0 427.7 jit_solution(11075137113260490227)
XLA Ops:
  7.2 2.9 collective-permute-start
  10.2 2.9 fusion.6
  13.0 42.2 %collective-permute-done = bf16[1,512,2048]{2,1,0:T(8,128)(2,1)S(1)} collective-permute-done((bf16[1,512,2048]{2,1,0:T(8,128)(2,1)}, bf16[1,512,2048]{2,1,0:T(8,128)(2,1)S(1)}, u32[]{:S(2)}, u32[]{:S(2)}) %collective-permute-start) | collective-permute-done | bytes 2097184 | tf_op jit(solution)/shard_map/ppermute | solution.py:10
  55.2 1.3 fusion.11
  56.5 1.5 pad_maximum_fusion
  58.1 95.0 %all-gather.5.cloned.1.call-done = f32[16,1,512,512]{3,2,1,0:T(8,128)} async-done(((f32[2,1,512,512]{3,2,1,0:T(8,128)}), f32[16,1,512,512]{3,2,1,0:T(8,128)}) %all-gather.5.cloned.1.call-update) | async-done | bytes 16777232 | tf_op jit(solution)/shard_map/all_gather | solution.py:38
  153.0 9.4 %bitcast_reduce_fusion = f32[2,512,512]{2,1,0:T(8,128)} fusion(f32[8,2,512,512]{3,2,1,0:T(8,128)} %bitcast.31), kind=kLoop, calls=%fused_computation.1 | loop fusion | flops 3670016 | bytes 18874368 | tf_op jit(solution)/shard_map/reduce_sum | solution.py:38
  162.5 1.7 constant_dynamic-slice_fusion
  164.2 189.2 %all-gather.7.cloned.1.call-done = f32[128,64,512]{2,1,0:T(8,128)} async-done(((f32[2,64,512]{2,1,0:T(8,128)}), f32[128,64,512]{2,1,0:T(8,128)}) %all-gather.7.cloned.1.call-update) | async-done | bytes 16777232 | tf_op jit(solution)/shard_map/all_gather | solution.py:15
  353.3 65.8 %while.10 = (s32[]{:T(128)}, f32[2,64,512]{2,1,0:T(8,128)S(1)}, s32[]{:T(128)}, f32[64,2,64,512]{3,2,1,0:T(8,128)}, s32[]{:T(128)}, /*index=5*/s32[]{:T(128)}, s32[]{:T(128)}) while((s32[]{:T(128)}, f32[2,64,512]{2,1,0:T(8,128)S(1)}, s32[]{:T(128)}, f32[64,2,64,512]{3,2,1,0:T(8,128)}, s32[]{:T(128)}, /*index=5*/s32[]{:T(128)}, s32[]{:T(128)}) %tuple.30), condition=%wide.region_2.3_spmd, body=%wide.region_1.0_spmd.sunk | while | flops 65541 | bytes 786555 | solution.py:21
  353.4 1.0 bitcast_add_fusion.2
  354.4 1.0 bitcast_add_fusion.2
  355.5 1.0 bitcast_add_fusion.2
  356.5 1.0 bitcast_add_fusion.2
  357.5 1.0 bitcast_add_fusion.2
  358.6 1.0 bitcast_add_fusion.2
  359.6 1.0 bitcast_add_fusion.2
  360.7 1.0 bitcast_add_fusion.2
  361.7 1.0 bitcast_add_fusion.2
  363.8 1.0 bitcast_add_fusion.2
  365.9 1.0 bitcast_add_fusion.2
  377.4 1.0 bitcast_add_fusion.2
  379.5 1.0 bitcast_add_fusion.2
  381.6 1.0 bitcast_add_fusion.2
  383.6 1.0 bitcast_add_fusion.2
  385.7 1.0 bitcast_add_fusion.2
  397.2 1.0 bitcast_add_fusion.2
  399.3 1.0 bitcast_add_fusion.2
  401.4 1.0 bitcast_add_fusion.2
  403.5 1.0 bitcast_add_fusion.2
  405.6 1.0 bitcast_add_fusion.2
  417.1 1.0 bitcast_add_fusion.2
  (50 shorter events, 43.8 us)
Async XLA Ops:
  7.2 3.0 copy-start
  7.2 145.9 %all-gather.5.cloned.1.call-start = ((), (), s32[]{:S(2)}) async-start(), calls=%async_computation | async-start | bytes 18874368 | tf_op jit(solution)/shard_map/all_gather | solution.py:38
  7.2 48.0 %collective-permute-start = (bf16[1,512,2048]{2,1,0:T(8,128)(2,1)}, bf16[1,512,2048]{2,1,0:T(8,128)(2,1)S(1)}, u32[]{:S(2)}, u32[]{:S(2)}) collective-permute-start(bf16[1,512,2048]{2,1,0:T(8,128)(2,1)} %param.5), channel_id=1, source_target_pairs={{8,0},{16,8},{24,16},{32,24},{40,32},{48,40},{56,48},{64,56},{72,6... | collective-permute-start | bytes 6291464 | tf_op jit(solution)/shard_map/ppermute | solution.py:10
  58.0 295.3 %all-gather.7.cloned.1.call-start = ((), (), s32[]{:S(2)}) async-start(), calls=%async_computation.1 | async-start | bytes 17039360 | tf_op jit(solution)/shard_map/all_gather | solution.py:15
Sparse Core Ops, SparseCore 0:
  58.2 94.8 all-gather.4
  164.3 188.9 all-gather.6
